TPU v7x, 128 devices: a whole 4x4x4 slice. The times are simulated.
128 devices in a mesh: wide: 16 (over z, y), narrow: 8 (over x, core).
Axes of the slice: x: 4, y: 4, z: 4, core: 2. Of those that a mesh axis runs over, the one named last changes fastest.
Arguments:
- state: bfloat16 [4096, 1024, 128], P(('wide', 'narrow')), may hold values from -6 to 6
- group_of: int32 [4096], replicated, may hold values from 0 to 4095, as said below
- w_in: bfloat16 [1024, 1024], replicated, may hold values from -0.1875 to 0.1875
- w_out: bfloat16 [1024, 1024], replicated, may hold values from -0.1875 to 0.1875
- w_flux: bfloat16 [32, 1024], replicated, may hold values from -0.1875 to 0.1875
- owner: int32 [524288, 1], P(('wide', 'narrow')), may hold values from 0 to 127; in each aligned block of 4096 rows (0 to 4095, 4096 to 8191, ...) at most 64 rows name the same one
- ocean_slot: int32 [524288], P(('wide', 'narrow')), may hold values from 0 to 511
- remap_weight: float32 [524288], P(('wide', 'narrow')), may hold values from 0.25 to 4
Outputs:
- new_state: bfloat16 [4096, 1024, 128], P(('wide', 'narrow'))
- ocean: float32 [32, 65536], P(None, ('wide', 'narrow'))
Inputs may be any that keep to these rules, and one draw needn't show every extreme that they name: group_of is a permutation of the blocks. Block p = ((w * 8 + n) * 32 + s) keeps n and s; for each n exactly 8 slots s move, each to wide index (w + c) modulo the wide size with a nonzero c of its own, and all other blocks stay.
All inputs are finite; a program needn't handle non-finite values.
Results may differ from a plain program's by a relative error of at most 0.0044.
Values may be sent and summed in bfloat16 or wider, within the bound.
A program may use at most 192 MiB of HBM per device.

v0:
```python
import functools

import jax
import jax.numpy as jnp
from jax import lax
from jax.experimental import pallas as pl
from jax.experimental.pallas import tpu as pltpu
from jax.sharding import PartitionSpec as P

F32, BF16, I32 = jnp.float32, jnp.bfloat16, jnp.int32
MESH = pl.DeviceIdType.MESH
NT = (((1,), (1,)), ((), ()))

BLOCKS, DEPTH, COLS = 32, 1024, 128
NFLUX, SLOTS = 32, 512
WIDE, NARROW, SIDE = 16, 8, 4
DEVICES = WIDE * NARROW
MOVE, STAY = 8, 24
GROUP = 4
CHUNK = 256
ITEMS = (
    (1, 0), (3, 0), (0, 1), (0, 3), (2, 2), (1, 1), (3, 3), (1, 3),
    (3, 1), (2, 1), (2, 3), (1, 2), (3, 2), (2, 0), (0, 2),
)
CODES = tuple(dz * SIDE + dy for dy, dz in ITEMS)
EARLY = 11
PARTS = 4


def silu(v):
    return v / (1.0 + jnp.exp(-v))


def main_kernel(
    group_of, state, w_in_hbm, w_out_hbm, w_flux, owner, slot, weight,
    pool, ocean, sel,
    xs, ys, send, w_in, w_out, hid, fm, fs, fp, key, jrank, bmat, msg, n1, w2, sl, s1, s1t, s2, hot,
    code_t, slot_t, next_t, rank_t, order_t, local_t,
    load_sem, pool_sem, big_s, big_r, fl_s, fl_r, na_s, na_r, wi_s, wi_r, sn_s, sn_r, sw_s, sw_r,
):
    w, n = lax.axis_index("wide"), lax.axis_index("narrow")
    y, z = lax.rem(w, SIDE), lax.div(w, SIDE)
    loads = [
        pltpu.make_async_copy(w_in_hbm, w_in, load_sem.at[0]),
        pltpu.make_async_copy(w_out_hbm, w_out, load_sem.at[9]),
    ]
    for i in range(8):
        loads.append(
            pltpu.make_async_copy(
                state.at[pl.ds(4 * i, 4)], xs.at[pl.ds(4 * i, 4)], load_sem.at[1 + i]
            )
        )
    loads[0].start()
    for c in loads[2:]:
        c.start()
    loads[1].start()

    def target(p):
        dy, dz = ITEMS[p]
        return (lax.rem(z + dz, SIDE) * SIDE + lax.rem(y + dy, SIDE), n)

    wide_peers = [(lax.rem(w + d, WIDE), n) for d in range(1, WIDE)]
    narrow_peers = [(w, lax.rem(n + d, NARROW)) for d in range(1, NARROW)]
    barrier = pltpu.get_barrier_semaphore()
    for peer in wide_peers + narrow_peers:
        pl.semaphore_signal(barrier, inc=1, device_id=peer, device_id_type=MESH)

    base_row = (w * NARROW + n) * BLOCKS

    def scan_slots(s, found):
        t = lax.div(group_of[base_row + s], NARROW * BLOCKS)
        dy = lax.rem(lax.rem(t, SIDE) - y + SIDE, SIDE)
        dz = lax.rem(lax.div(t, SIDE) - z + SIDE, SIDE)
        src = lax.rem(2 * w - t + 2 * WIDE, WIDE)
        ry = lax.rem(y - lax.rem(src, SIDE) + SIDE, SIDE)
        rz = lax.rem(z - lax.div(src, SIDE) + SIDE, SIDE)
        code = dz * SIDE + dy
        code_t[s] = code
        sel[s] = STAY + rz * SIDE + ry
        return tuple(jnp.where(code == CODES[p], s, found[p]) for p in range(15))

    found = lax.fori_loop(0, BLOCKS, scan_slots, (jnp.int32(-1),) * 15)
    nxt = jnp.int32(15)
    slot_t[15] = jnp.int32(0)
    next_t[15] = jnp.int32(15)
    next_t[16] = jnp.int32(15)
    for p in reversed(range(15)):
        nxt = jnp.where(found[p] >= 0, p, nxt)
        next_t[p] = nxt
        slot_t[p] = jnp.maximum(found[p], 0)
    count = jnp.int32(0)
    for p in range(15):
        rank_t[p] = jnp.minimum(count, MOVE - 1)
        count = count + jnp.where(found[p] >= 0, 1, 0)

    def walk_movers(k, p):
        order_t[k] = slot_t[p]
        return next_t[p + 1]

    lax.fori_loop(0, MOVE, walk_movers, next_t[0])

    def back_locals(i, nx):
        s = BLOCKS - 1 - i
        nx = jnp.where(code_t[s] == 0, s, nx)
        local_t[s] = nx
        return nx

    local_t[BLOCKS] = jnp.int32(BLOCKS - 1)
    lax.fori_loop(0, BLOCKS, back_locals, jnp.int32(BLOCKS - 1))

    def number_locals(s, cnt):
        stays = code_t[s] == 0
        sel[s] = jnp.where(stays, jnp.minimum(cnt, STAY - 1), sel[s])
        return cnt + jnp.where(stays, 1, 0)

    lax.fori_loop(0, BLOCKS, number_locals, jnp.int32(0))

    def walk_locals(k, s):
        order_t[MOVE + k] = s
        return local_t[s + 1]

    lax.fori_loop(0, STAY, walk_locals, local_t[0])

    sub = lax.broadcasted_iota(I32, (COLS, COLS), 0)
    lane = lax.broadcasted_iota(I32, (COLS, COLS), 1)
    before = jnp.where(sub < lane, 1.0, 0.0).astype(BF16)
    ones = jnp.full((COLS, COLS), 1.0, BF16)

    def place(s, carry):
        base, table = carry
        o = owner[s]
        row = (o & (NARROW - 1)) * WIDE + (o >> 3)
        member = jnp.where(sub == row, 1.0, 0.0)
        member16 = member.astype(BF16)
        ahead = jnp.dot(member16, before, preferred_element_type=F32) + base
        rank = jnp.sum(ahead * member, axis=0, keepdims=True).astype(I32)
        base = base + jnp.dot(member16, ones, preferred_element_type=F32)
        key[s] = row * 16 + (rank >> 2)
        jrank[s] = rank & 3
        cell = (slot[s] - SLOTS // 2).astype(F32)
        ranked = jnp.where(sub == rank, cell, 0.0).astype(BF16)
        table = table + lax.dot_general(member16, ranked, NT, preferred_element_type=F32)
        return base, table

    zero = jnp.zeros((COLS, COLS), F32)
    _, table = lax.fori_loop(0, BLOCKS, place, (zero, zero))
    sl[...] = table.reshape(NARROW, WIDE, COLS)

    pl.semaphore_wait(barrier, len(wide_peers) + len(narrow_peers))

    slot_narrow = []
    for d in range(1, NARROW):
        p = lax.rem(n + d, NARROW)
        c = pltpu.make_async_remote_copy(
            sl.at[p], s1.at[n], sn_s.at[d], sn_r.at[d], device_id=(w, p), device_id_type=MESH
        )
        c.start()
        slot_narrow.append(c)
    s1[n] = sl[n]

    def big(p, part=None):
        rows = pl.ds(0, DEPTH) if part is None else pl.ds(part * CHUNK, CHUNK)
        return pltpu.make_async_remote_copy(
            send.at[p, rows],
            pool.at[STAY + CODES[p], rows],
            big_s.at[p],
            big_r.at[p],
            device_id=target(p),
            device_id_type=MESH,
        )

    def flux_copy(p):
        return pltpu.make_async_remote_copy(
            fs.at[p], fp.at[STAY + CODES[p]], fl_s.at[p], fl_r.at[p],
            device_id=target(p), device_id_type=MESH,
        )

    def fill(ps):
        for p in ps:
            fs[p] = fm[rank_t[p]]
        for p in ps:
            send[p] = ys[rank_t[p]]

    def send_big(ps):
        for part in range(PARTS):
            for p in ps:
                big(p, part).start()

    def to_pool(q):
        return pltpu.make_async_copy(
            ys.at[pl.ds(GROUP * q, GROUP)],
            pool.at[pl.ds(GROUP * q - MOVE, GROUP)],
            pool_sem.at[q],
        )

    slot_wide = []
    for d in range(1, WIDE):
        q = lax.rem(w + d, WIDE)
        slot_wide.append(
            pltpu.make_async_remote_copy(
                s1t.at[q], s2.at[w], sw_s.at[d], sw_r.at[d], device_id=(q, n), device_id_type=MESH
            )
        )

    for c in loads:
        c.wait()

    @pl.loop(0, BLOCKS // GROUP)
    def _(q):
        x = jnp.concatenate([xs[order_t[GROUP * q + g]] for g in range(GROUP)], axis=1)
        for m in range(DEPTH // CHUNK):
            rows = pl.ds(m * CHUNK, CHUNK)
            hid[rows, :] = silu(
                jnp.dot(w_in[rows, :], x, preferred_element_type=F32)
            ).astype(BF16)
        h = hid[...]
        f = jnp.dot(w_flux[...], h, preferred_element_type=F32)

        @pl.when(q < 2)
        def _():
            for g in range(GROUP):
                fm[GROUP * q + g] = f[:, g * COLS : (g + 1) * COLS]

        @pl.when(q >= 2)
        def _():
            for g in range(GROUP):
                fp[GROUP * q - MOVE + g] = f[:, g * COLS : (g + 1) * COLS]

        for m in range(DEPTH // CHUNK):
            rows = pl.ds(m * CHUNK, CHUNK)
            fresh = jnp.dot(w_out[rows, :], h, preferred_element_type=F32)
            fresh = (fresh + x[m * CHUNK : (m + 1) * CHUNK].astype(F32)).astype(BF16)
            for g in range(GROUP):
                ys[GROUP * q + g, rows] = fresh[:, g * COLS : (g + 1) * COLS]

        @pl.when(q == 0)
        def _():
            fill(range(4))
            for p in range(4):
                flux_copy(p).start()
            send_big(range(4))

        @pl.when(q == 1)
        def _():
            fill(range(4, 15))
            for p in range(4, 15):
                flux_copy(p).start()
            send_big(range(4, EARLY))

        @pl.when(q == 2)
        def _():
            for c in slot_narrow:
                c.wait()
            for p in range(NARROW):
                s1t[:, p, :] = s1[p]
            s2[w] = s1t[w]
            for c in slot_wide:
                c.start()

        @pl.when(q >= 3)
        def _():
            to_pool(q - 1).start()

    for p in range(15):
        flux_copy(p).wait()
    to_pool(BLOCKS // GROUP - 1).start()

    @pl.loop(0, BLOCKS)
    def _(s):
        f = fp[sel[s]] * weight[s]
        j = jrank[s]
        spread = jnp.concatenate([jnp.where(j == k, f, 0.0) for k in range(4)], axis=0)
        bmat[s] = spread.astype(BF16)

    STEP = 512
    row_id = lax.broadcasted_iota(I32, (STEP, COLS), 0)

    @pl.loop(0, 2048 // STEP)
    def _(r):
        acc = jnp.zeros((STEP, COLS), F32)
        for b in range(0, BLOCKS, 4):
            pick = jnp.concatenate(
                [
                    jnp.where(row_id == key[b + g] - r * STEP, 1.0, 0.0).astype(BF16)
                    for g in range(4)
                ],
                axis=1,
            )
            vals = jnp.concatenate([bmat[b + g] for g in range(4)], axis=1)
            acc = acc + lax.dot_general(pick, vals, NT, preferred_element_type=F32)
        msg[pl.ds(2 * r, 2)] = acc.astype(BF16).reshape(2, WIDE, 16, COLS)

    narrow = []
    for d in range(1, NARROW):
        p = lax.rem(n + d, NARROW)
        c = pltpu.make_async_remote_copy(
            msg.at[p], n1.at[:, n], na_s.at[d], na_r.at[d], device_id=(w, p), device_id_type=MESH
        )
        c.start()
        narrow.append(c)
    n1[:, n] = msg[n]
    for c in slot_wide:
        c.wait()
    for c in narrow:
        c.wait()
    wide = []
    for d in range(1, WIDE):
        q = lax.rem(w + d, WIDE)
        c = pltpu.make_async_remote_copy(
            n1.at[q], w2.at[w], wi_s.at[d], wi_r.at[d], device_id=(q, n), device_id_type=MESH
        )
        c.start()
        wide.append(c)
    w2[w] = n1[w]
    send_big(range(EARLY, 15))

    cells = s2[...].reshape(DEVICES, COLS).astype(BF16)
    ROWS = 256
    sub2 = lax.broadcasted_iota(I32, (ROWS, COLS), 0)
    lane2 = lax.broadcasted_iota(I32, (ROWS, COLS), 1)

    @pl.loop(0, 2048 // ROWS)
    def _(r):
        own = jnp.where(lane2 == r * (ROWS // 16) + (sub2 >> 4), 1.0, 0.0).astype(BF16)
        mine = jnp.dot(own, cells, preferred_element_type=F32)
        for j in range(4):
            one = jnp.where(lane2 == 4 * (sub2 & 15) + j, mine, 0.0).astype(BF16)
            cell = jnp.dot(one, ones, preferred_element_type=F32)
            cell = cell.astype(I32) + SLOTS // 2
            for k in range(SLOTS // COLS):
                hot[j, pl.ds(r * ROWS, ROWS), k * COLS : (k + 1) * COLS] = jnp.where(
                    cell == lane2 + k * COLS, 1.0, 0.0
                ).astype(BF16)

    for c in wide:
        c.wait()
    eye = jnp.where(sub == lane, 1.0, 0.0).astype(BF16)
    vals = w2[...].reshape(2048, COLS)
    turned = lax.dot_general(eye, vals, NT, preferred_element_type=F32).astype(BF16)
    total = jnp.zeros((NFLUX, SLOTS), F32)
    for j in range(4):
        total = total + jnp.dot(
            turned[j * NFLUX : (j + 1) * NFLUX], hot[j], preferred_element_type=F32
        )
    ocean[...] = total

    for q in range(2, BLOCKS // GROUP):
        to_pool(q).wait()
    for p in range(15):
        big(p).wait()


def final_kernel(sel, pool, out, buf, in_sem, out_sem):
    def fetch(s):
        return pltpu.make_async_copy(pool.at[sel[s]], buf.at[s], in_sem.at[s])

    def put(s):
        return pltpu.make_async_copy(buf.at[s], out.at[s], out_sem.at[s])

    for s in range(BLOCKS):
        fetch(s).start()
    for s in range(BLOCKS):
        fetch(s).wait()
        put(s).start()
    for s in range(BLOCKS):
        put(s).wait()


def per_device(state, group_of, w_in, w_out, w_flux, owner, ocean_slot, remap_weight):
    vmem, anys, smem = (
        pl.BlockSpec(memory_space=pltpu.VMEM),
        pl.BlockSpec(memory_space=pl.ANY),
        pl.BlockSpec(memory_space=pltpu.SMEM),
    )
    dma = pltpu.SemaphoreType.DMA
    pool, ocean, sel = pl.pallas_call(
        main_kernel,
        out_shape=(
            jax.ShapeDtypeStruct((STAY + WIDE, DEPTH, COLS), BF16),
            jax.ShapeDtypeStruct((NFLUX, SLOTS), F32),
            jax.ShapeDtypeStruct((BLOCKS,), I32),
        ),
        in_specs=[smem, anys, anys, anys, vmem, vmem, vmem, vmem],
        out_specs=(anys, vmem, smem),
        scratch_shapes=[
            pltpu.VMEM((BLOCKS, DEPTH, COLS), BF16),
            pltpu.VMEM((BLOCKS, DEPTH, COLS), BF16),
            pltpu.VMEM((15, DEPTH, COLS), BF16),
            pltpu.VMEM((DEPTH, DEPTH), BF16),
            pltpu.VMEM((DEPTH, DEPTH), BF16),
            pltpu.VMEM((DEPTH, GROUP * COLS), BF16),
            pltpu.VMEM((MOVE, NFLUX, COLS), F32),
            pltpu.VMEM((15, NFLUX, COLS), F32),
            pltpu.VMEM((STAY + WIDE, NFLUX, COLS), F32),
            pltpu.VMEM((BLOCKS, 1, COLS), I32),
            pltpu.VMEM((BLOCKS, 1, COLS), I32),
            pltpu.VMEM((BLOCKS, COLS, COLS), BF16),
            pltpu.VMEM((NARROW, WIDE, 16, COLS), BF16),
            pltpu.VMEM((WIDE, NARROW, 16, COLS), BF16),
            pltpu.VMEM((WIDE, NARROW, 16, COLS), BF16),
            pltpu.VMEM((NARROW, WIDE, COLS), F32),
            pltpu.VMEM((NARROW, WIDE, COLS), F32),
            pltpu.VMEM((WIDE, NARROW, COLS), F32),
            pltpu.VMEM((WIDE, NARROW, COLS), F32),
            pltpu.VMEM((4, 2048, SLOTS), BF16),
            pltpu.SMEM((BLOCKS,), I32),
            pltpu.SMEM((16,), I32),
            pltpu.SMEM((17,), I32),
            pltpu.SMEM((15,), I32),
            pltpu.SMEM((BLOCKS,), I32),
            pltpu.SMEM((BLOCKS + 1,), I32),
            dma((10,)),
            dma((8,)),
            dma((15,)),
            dma((15,)),
            dma((15,)),
            dma((15,)),
            dma((NARROW,)),
            dma((NARROW,)),
            dma((WIDE,)),
            dma((WIDE,)),
            dma((NARROW,)),
            dma((NARROW,)),
            dma((WIDE,)),
            dma((WIDE,)),
        ],
        compiler_params=pltpu.CompilerParams(
            collective_id=1, has_side_effects=True, vmem_limit_bytes=60 * 2**20
        ),
        name="physics",
    )(
        group_of,
        state,
        w_in,
        w_out,
        w_flux,
        owner.reshape(BLOCKS, 1, COLS),
        ocean_slot.reshape(BLOCKS, 1, COLS),
        remap_weight.reshape(BLOCKS, 1, COLS),
    )
    new_state = pl.pallas_call(
        final_kernel,
        out_shape=jax.ShapeDtypeStruct((BLOCKS, DEPTH, COLS), BF16),
        in_specs=[smem, anys],
        out_specs=anys,
        scratch_shapes=[
            pltpu.VMEM((BLOCKS, DEPTH, COLS), BF16),
            dma((BLOCKS,)),
            dma((BLOCKS,)),
        ],
        name="assemble",
    )(sel, pool)
    return new_state, ocean


def solution(mesh):
    rows = P(("wide", "narrow"))
    in_specs = (P(("wide", "narrow"), None, None), P(), P(), P(), P(), P(("wide", "narrow"), None), rows, rows)
    out_specs = (P(("wide", "narrow"), None, None), P(None, ("wide", "narrow")))
    return jax.shard_map(
        per_device, mesh=mesh, in_specs=in_specs, out_specs=out_specs, check_vma=False
    )
```

profile of v0, /device:TPU:1, one launch (start us, length us, event | category | flops | bytes accessed | tf_op | source)
XLA Modules:
  0.0 97.8 jit_solution(16035165221761382942)
XLA Ops:
  0.6 88.7 %physics.1 = (bf16[40,1024,128]{2,1,0:T(8,128)(2,1)}, f32[32,512]{1,0:T(8,128)}, s32[32]{0:T(128)}) custom-call(s32[4096]{0:T(1024)} %group_of.1, bf16[32,1024,128]{2,1,0:T(8,128)(2,1)} %state.1, bf16[1024,1024]{1,0:T(8,128)(2,1)} %w_in_hbm.1, bf16[1024,1024]{1,0:T(8,128)(2,1)} %w_out_hbm.1, bf16[32,1024]{1,0:T(8,128)(2,1)} %w_flux.1, ...), custom_call_target="tpu_custom_call" | custom-call | tf_op jit(solution)/shard_map/physics/pallas_call | solution.py:376
  89.3 0.0 copy-start
  89.3 7.8 %assemble.1 = bf16[32,1024,128]{2,1,0:T(8,128)(2,1)} custom-call(s32[32]{0:T(128)} %get-tuple-element.5.sel, bf16[40,1024,128]{2,1,0:T(8,128)(2,1)} %get-tuple-element.6.pool), custom_call_target="tpu_custom_call" | custom-call | tf_op jit(solution)/shard_map/assemble/pallas_call | solution.py:441
  97.2 0.0 copy-done
  97.2 0.6 copy.11
Async XLA Ops:
  89.3 7.8 %copy-start = (f32[32,512]{1,0:T(8,128)S(1)}, f32[32,512]{1,0:T(8,128)}, u32[]{:S(2)}) copy-start(f32[32,512]{1,0:T(8,128)} %get-tuple-element.11) | copy-start | bytes 196612
where the time goes:
time: 98 us; the launch traced here: 97.8 us
  Pallas kernels  96.5 us (98%)
    pallas_call x1, Pallas kernels, per_device(): pl.pallas_call(main_kernel, out_shape=(jax.ShapeDtypeStruct((STAY + WIDE,...  88.7 us
    pallas_call x1, Pallas kernels, per_device(): pl.pallas_call(final_kernel, out_shape=jax.ShapeDtypeStruct((BLOCKS, DEPT...  7.82 us

commit v1 on v0

--- a/solution.py
+++ b/solution.py
@@ -23,8 +23,12 @@
     (3, 1), (2, 1), (2, 3), (1, 2), (3, 2), (2, 0), (0, 2),
 )
 CODES = tuple(dz * SIDE + dy for dy, dz in ITEMS)
-EARLY = 11
 PARTS = 4
+ORDER = [(p, part) for part in range(PARTS) for p in range(4)]
+ORDER += [(p, part) for part in range(PARTS) for p in range(4, 15)]
+SENT = (16, 24, 28, 32, 36, 40, 44, 48)
+SENT_SORT = 52
+SENT_NARROW = 56
 
 
 def silu(v):
@@ -34,9 +38,9 @@
 def main_kernel(
     group_of, state, w_in_hbm, w_out_hbm, w_flux, owner, slot, weight,
     pool, ocean, sel,
-    xs, ys, send, w_in, w_out, hid, fm, fs, fp, key, jrank, bmat, msg, n1, w2, sl, s1, s1t, s2, hot,
+    xs, ys, send, w_in, w_out, hid, fm, fs, fp, fr, key, jrank, bmat, msg, n1, w2, sl, s1, s1t, s2, hot,
     code_t, slot_t, next_t, rank_t, order_t, local_t,
-    load_sem, pool_sem, big_s, big_r, fl_s, fl_r, na_s, na_r, wi_s, wi_r, sn_s, sn_r, sw_s, sw_r,
+    load_sem, big_s, big_r, fl_s, fl_r, na_s, na_r, wi_s, wi_r, sn_s, sn_r, sw_s, sw_r,
 ):
     w, n = lax.axis_index("wide"), lax.axis_index("narrow")
     y, z = lax.rem(w, SIDE), lax.div(w, SIDE)
@@ -126,27 +130,33 @@
     before = jnp.where(sub < lane, 1.0, 0.0).astype(BF16)
     ones = jnp.full((COLS, COLS), 1.0, BF16)
 
-    def place(s, carry):
+    def place(i, carry):
         base, table = carry
-        o = owner[s]
-        row = (o & (NARROW - 1)) * WIDE + (o >> 3)
-        member = jnp.where(sub == row, 1.0, 0.0)
-        member16 = member.astype(BF16)
-        ahead = jnp.dot(member16, before, preferred_element_type=F32) + base
-        rank = jnp.sum(ahead * member, axis=0, keepdims=True).astype(I32)
-        base = base + jnp.dot(member16, ones, preferred_element_type=F32)
-        key[s] = row * 16 + (rank >> 2)
-        jrank[s] = rank & 3
-        cell = (slot[s] - SLOTS // 2).astype(F32)
-        ranked = jnp.where(sub == rank, cell, 0.0).astype(BF16)
-        table = table + lax.dot_general(member16, ranked, NT, preferred_element_type=F32)
+        for g in range(4):
+            s = 4 * i + g
+            o = owner[s]
+            row = (o & (NARROW - 1)) * WIDE + (o >> 3)
+            member = jnp.where(sub == row, 1.0, 0.0)
+            member16 = member.astype(BF16)
+            ahead = jnp.dot(member16, before, preferred_element_type=F32)
+            count = jnp.dot(member16, ones, preferred_element_type=F32)
+            rank = jnp.sum((ahead + base) * member, axis=0, keepdims=True).astype(I32)
+            base = base + count
+            key[s] = row * 16 + (rank >> 2)
+            jrank[s] = rank & 3
+            cell = (slot[s] - SLOTS // 2).astype(F32)
+            ranked = jnp.where(sub == rank, cell, 0.0).astype(BF16)
+            table = table + lax.dot_general(member16, ranked, NT, preferred_element_type=F32)
         return base, table
 
-    zero = jnp.zeros((COLS, COLS), F32)
-    _, table = lax.fori_loop(0, BLOCKS, place, (zero, zero))
-    sl[...] = table.reshape(NARROW, WIDE, COLS)
-
-    pl.semaphore_wait(barrier, len(wide_peers) + len(narrow_peers))
+    def slots_out():
+        zero = jnp.zeros((COLS, COLS), F32)
+        _, table = lax.fori_loop(0, BLOCKS // 4, place, (zero, zero))
+        sl[...] = table.reshape(NARROW, WIDE, COLS)
+        for c in slot_narrow:
+            c.start()
+        s1[n] = sl[n]
+
 
     slot_narrow = []
     for d in range(1, NARROW):
@@ -154,9 +164,7 @@
         c = pltpu.make_async_remote_copy(
             sl.at[p], s1.at[n], sn_s.at[d], sn_r.at[d], device_id=(w, p), device_id_type=MESH
         )
-        c.start()
         slot_narrow.append(c)
-    s1[n] = sl[n]
 
     def big(p, part=None):
         rows = pl.ds(0, DEPTH) if part is None else pl.ds(part * CHUNK, CHUNK)
@@ -171,27 +179,19 @@
 
     def flux_copy(p):
         return pltpu.make_async_remote_copy(
-            fs.at[p], fp.at[STAY + CODES[p]], fl_s.at[p], fl_r.at[p],
+            fs.at[p], fr.at[CODES[p]], fl_s.at[p], fl_r.at[p],
             device_id=target(p), device_id_type=MESH,
         )
 
     def fill(ps):
         for p in ps:
-            fs[p] = fm[rank_t[p]]
+            fs[p] = fm[rank_t[p]].astype(BF16)
         for p in ps:
             send[p] = ys[rank_t[p]]
 
-    def send_big(ps):
-        for part in range(PARTS):
-            for p in ps:
-                big(p, part).start()
-
-    def to_pool(q):
-        return pltpu.make_async_copy(
-            ys.at[pl.ds(GROUP * q, GROUP)],
-            pool.at[pl.ds(GROUP * q - MOVE, GROUP)],
-            pool_sem.at[q],
-        )
+    def send_big(first, last):
+        for p, part in ORDER[first:last]:
+            big(p, part).start()
 
     slot_wide = []
     for d in range(1, WIDE):
@@ -230,24 +230,34 @@
             rows = pl.ds(m * CHUNK, CHUNK)
             fresh = jnp.dot(w_out[rows, :], h, preferred_element_type=F32)
             fresh = (fresh + x[m * CHUNK : (m + 1) * CHUNK].astype(F32)).astype(BF16)
-            for g in range(GROUP):
-                ys[GROUP * q + g, rows] = fresh[:, g * COLS : (g + 1) * COLS]
+
+            @pl.when(q < 2)
+            def _(rows=rows, fresh=fresh):
+                for g in range(GROUP):
+                    ys[GROUP * q + g, rows] = fresh[:, g * COLS : (g + 1) * COLS]
+
+            @pl.when(q >= 2)
+            def _(rows=rows, fresh=fresh):
+                for g in range(GROUP):
+                    pool[GROUP * q - MOVE + g, rows] = fresh[:, g * COLS : (g + 1) * COLS]
 
         @pl.when(q == 0)
         def _():
             fill(range(4))
+            pl.semaphore_wait(barrier, len(wide_peers) + len(narrow_peers))
             for p in range(4):
                 flux_copy(p).start()
-            send_big(range(4))
+            send_big(0, SENT[0])
 
         @pl.when(q == 1)
         def _():
             fill(range(4, 15))
             for p in range(4, 15):
                 flux_copy(p).start()
-            send_big(range(4, EARLY))
-
-        @pl.when(q == 2)
+            send_big(SENT[0], SENT[1])
+            slots_out()
+
+        @pl.when(q == 3)
         def _():
             for c in slot_narrow:
                 c.wait()
@@ -257,13 +267,18 @@
             for c in slot_wide:
                 c.start()
 
-        @pl.when(q >= 3)
-        def _():
-            to_pool(q - 1).start()
+        for step in range(2, BLOCKS // GROUP):
+
+            @pl.when(q == step)
+            def _(step=step):
+                send_big(SENT[step - 1], SENT[step])
+
 
     for p in range(15):
         flux_copy(p).wait()
-    to_pool(BLOCKS // GROUP - 1).start()
+    fp[STAY:] = fr[...].astype(F32)
+
+    send_big(SENT[-1], SENT_SORT)
 
     @pl.loop(0, BLOCKS)
     def _(s):
@@ -272,37 +287,43 @@
         spread = jnp.concatenate([jnp.where(j == k, f, 0.0) for k in range(4)], axis=0)
         bmat[s] = spread.astype(BF16)
 
-    STEP = 512
-    row_id = lax.broadcasted_iota(I32, (STEP, COLS), 0)
-
-    @pl.loop(0, 2048 // STEP)
+    HALF = WIDE * 16
+    row_id = lax.broadcasted_iota(I32, (2 * HALF, COLS), 0)
+
+    def narrow_copy(d):
+        p = lax.rem(n + d, NARROW)
+        return pltpu.make_async_remote_copy(
+            msg.at[p], n1.at[:, n], na_s.at[d], na_r.at[d], device_id=(w, p), device_id_type=MESH
+        )
+
+    @pl.loop(0, NARROW // 2)
     def _(r):
-        acc = jnp.zeros((STEP, COLS), F32)
+        d = 2 * r + 1
+        p0, p1 = lax.rem(n + d, NARROW), lax.rem(n + d + 1, NARROW)
+        wanted = row_id + jnp.where(row_id < HALF, p0 * HALF, (p1 - 1) * HALF)
+        acc = jnp.zeros((2 * HALF, COLS), F32)
         for b in range(0, BLOCKS, 4):
             pick = jnp.concatenate(
-                [
-                    jnp.where(row_id == key[b + g] - r * STEP, 1.0, 0.0).astype(BF16)
-                    for g in range(4)
-                ],
+                [jnp.where(wanted == key[b + g], 1.0, 0.0).astype(BF16) for g in range(4)],
                 axis=1,
             )
             vals = jnp.concatenate([bmat[b + g] for g in range(4)], axis=1)
             acc = acc + lax.dot_general(pick, vals, NT, preferred_element_type=F32)
-        msg[pl.ds(2 * r, 2)] = acc.astype(BF16).reshape(2, WIDE, 16, COLS)
-
-    narrow = []
-    for d in range(1, NARROW):
-        p = lax.rem(n + d, NARROW)
-        c = pltpu.make_async_remote_copy(
-            msg.at[p], n1.at[:, n], na_s.at[d], na_r.at[d], device_id=(w, p), device_id_type=MESH
-        )
-        c.start()
-        narrow.append(c)
+        both = acc.astype(BF16).reshape(2, WIDE, 16, COLS)
+        msg[p0] = both[0]
+        msg[p1] = both[1]
+        narrow_copy(d).start()
+
+        @pl.when(r < NARROW // 2 - 1)
+        def _():
+            narrow_copy(d + 1).start()
+
+    send_big(SENT_SORT, SENT_NARROW)
     n1[:, n] = msg[n]
     for c in slot_wide:
         c.wait()
-    for c in narrow:
-        c.wait()
+    for d in range(1, NARROW):
+        narrow_copy(d).wait()
     wide = []
     for d in range(1, WIDE):
         q = lax.rem(w + d, WIDE)
@@ -312,7 +333,7 @@
         c.start()
         wide.append(c)
     w2[w] = n1[w]
-    send_big(range(EARLY, 15))
+    send_big(SENT_NARROW, len(ORDER))
 
     cells = s2[...].reshape(DEVICES, COLS).astype(BF16)
     ROWS = 256
@@ -344,54 +365,50 @@
         )
     ocean[...] = total
 
-    for q in range(2, BLOCKS // GROUP):
-        to_pool(q).wait()
     for p in range(15):
         big(p).wait()
 
 
-def final_kernel(sel, pool, out, buf, in_sem, out_sem):
-    def fetch(s):
-        return pltpu.make_async_copy(pool.at[sel[s]], buf.at[s], in_sem.at[s])
-
+def final_kernel(sel, pool, cells, out, ocean, sem, cell_sem):
     def put(s):
-        return pltpu.make_async_copy(buf.at[s], out.at[s], out_sem.at[s])
+        return pltpu.make_async_copy(pool.at[sel[s]], out.at[s], sem.at[s])
 
     for s in range(BLOCKS):
-        fetch(s).start()
-    for s in range(BLOCKS):
-        fetch(s).wait()
         put(s).start()
+    last = pltpu.make_async_copy(cells, ocean, cell_sem)
+    last.start()
     for s in range(BLOCKS):
         put(s).wait()
+    last.wait()
 
 
 def per_device(state, group_of, w_in, w_out, w_flux, owner, ocean_slot, remap_weight):
-    vmem, anys, smem = (
+    vmem, hbm, smem = (
         pl.BlockSpec(memory_space=pltpu.VMEM),
-        pl.BlockSpec(memory_space=pl.ANY),
+        pl.BlockSpec(memory_space=pltpu.HBM),
         pl.BlockSpec(memory_space=pltpu.SMEM),
     )
     dma = pltpu.SemaphoreType.DMA
     pool, ocean, sel = pl.pallas_call(
         main_kernel,
         out_shape=(
-            jax.ShapeDtypeStruct((STAY + WIDE, DEPTH, COLS), BF16),
+            pltpu.VMEM((STAY + WIDE, DEPTH, COLS), BF16),
             jax.ShapeDtypeStruct((NFLUX, SLOTS), F32),
             jax.ShapeDtypeStruct((BLOCKS,), I32),
         ),
-        in_specs=[smem, anys, anys, anys, vmem, vmem, vmem, vmem],
-        out_specs=(anys, vmem, smem),
+        in_specs=[smem, hbm, hbm, hbm, vmem, vmem, vmem, vmem],
+        out_specs=(vmem, vmem, smem),
         scratch_shapes=[
             pltpu.VMEM((BLOCKS, DEPTH, COLS), BF16),
-            pltpu.VMEM((BLOCKS, DEPTH, COLS), BF16),
+            pltpu.VMEM((MOVE, DEPTH, COLS), BF16),
             pltpu.VMEM((15, DEPTH, COLS), BF16),
             pltpu.VMEM((DEPTH, DEPTH), BF16),
             pltpu.VMEM((DEPTH, DEPTH), BF16),
             pltpu.VMEM((DEPTH, GROUP * COLS), BF16),
             pltpu.VMEM((MOVE, NFLUX, COLS), F32),
-            pltpu.VMEM((15, NFLUX, COLS), F32),
+            pltpu.VMEM((15, NFLUX, COLS), BF16),
             pltpu.VMEM((STAY + WIDE, NFLUX, COLS), F32),
+            pltpu.VMEM((WIDE, NFLUX, COLS), BF16),
             pltpu.VMEM((BLOCKS, 1, COLS), I32),
             pltpu.VMEM((BLOCKS, 1, COLS), I32),
             pltpu.VMEM((BLOCKS, COLS, COLS), BF16),
@@ -410,7 +427,6 @@
             pltpu.SMEM((BLOCKS,), I32),
             pltpu.SMEM((BLOCKS + 1,), I32),
             dma((10,)),
-            dma((8,)),
             dma((15,)),
             dma((15,)),
             dma((15,)),
@@ -425,7 +441,7 @@
             dma((WIDE,)),
         ],
         compiler_params=pltpu.CompilerParams(
-            collective_id=1, has_side_effects=True, vmem_limit_bytes=60 * 2**20
+            collective_id=1, has_side_effects=True, vmem_limit_bytes=49 * 2**20
         ),
         name="physics",
     )(
@@ -438,19 +454,18 @@
         ocean_slot.reshape(BLOCKS, 1, COLS),
         remap_weight.reshape(BLOCKS, 1, COLS),
     )
-    new_state = pl.pallas_call(
+    return pl.pallas_call(
         final_kernel,
-        out_shape=jax.ShapeDtypeStruct((BLOCKS, DEPTH, COLS), BF16),
-        in_specs=[smem, anys],
-        out_specs=anys,
-        scratch_shapes=[
-            pltpu.VMEM((BLOCKS, DEPTH, COLS), BF16),
-            dma((BLOCKS,)),
-            dma((BLOCKS,)),
-        ],
+        out_shape=(
+            jax.ShapeDtypeStruct((BLOCKS, DEPTH, COLS), BF16),
+            jax.ShapeDtypeStruct((NFLUX, SLOTS), F32),
+        ),
+        in_specs=[smem, vmem, vmem],
+        out_specs=(hbm, hbm),
+        scratch_shapes=[dma((BLOCKS,)), dma],
+        compiler_params=pltpu.CompilerParams(vmem_limit_bytes=2 * 2**20),
         name="assemble",
-    )(sel, pool)
-    return new_state, ocean
+    )(sel, pool, ocean)
 
 
 def solution(mesh):

time: 98 us -> 80.2 us (0.82)
  Pallas kernels: 96.5 us -> 77.8 us
    pallas_call x2, Pallas kernels: 96.5 us -> 77.8 us  [the longest x1 73.7 us: per_device(): pl.pallas_call(main_kernel, out_shape=(pltpu.VMEM((STAY + WIDE, DEPTH, CO...]
where the time goes in v1:
time: 80.2 us; the launch traced here: 80 us
  Pallas kernels  77.8 us (97%)
  local copies, waits for them, and re-layouts  1.51 us (2%)
    pallas_call x1, Pallas kernels, per_device(): pl.pallas_call(main_kernel, out_shape=(pltpu.VMEM((STAY + WIDE, DEPTH, CO...  73.7 us
    pallas_call x1, Pallas kernels, per_device(): pl.pallas_call(final_kernel, out_shape=(jax.ShapeDtypeStruct((BLOCKS, DEP...  4.09 us

profile of v1, /device:TPU:1, one launch (start us, length us, event | category | flops | bytes accessed | tf_op | source)
XLA Modules:
  0.0 80.0 jit_solution(13642386527246919765)
XLA Ops:
  0.6 73.7 %physics.1 = (bf16[40,1024,128]{2,1,0:T(8,128)(2,1)S(1)}, f32[32,512]{1,0:T(8,128)}, s32[32]{0:T(128)}) custom-call(s32[4096]{0:T(1024)} %group_of.1, bf16[32,1024,128]{2,1,0:T(8,128)(2,1)} %state.1, bf16[1024,1024]{1,0:T(8,128)(2,1)} %w_in_hbm.1, bf16[1024,1024]{1,0:T(8,128)(2,1)} %w_out_hbm.1, bf16[32,1024]{1,0:T(8,128)(2,1)} %w_flux.1, ...), custom_call_target="tpu_custom_call" | custom-call | tf_op jit(solution)/shard_map/physics/pallas_call | solution.py:392
  74.4 0.0 copy-start
  74.4 0.8 %copy-done = f32[32,512]{1,0:T(8,128)S(1)} copy-done((f32[32,512]{1,0:T(8,128)S(1)}, f32[32,512]{1,0:T(8,128)}, u32[]{:S(2)}) %copy-start) | copy-done | bytes 65560
  75.2 0.0 copy-start.1
  75.2 0.7 copy-done.1
  75.9 4.1 %assemble.1 = (bf16[32,1024,128]{2,1,0:T(8,128)(2,1)}, f32[32,512]{1,0:T(8,128)}) custom-call(s32[32]{0:T(128)S(1)} %copy-done.1, bf16[40,1024,128]{2,1,0:T(8,128)(2,1)S(1)} %get-tuple-element.6.pool, f32[32,512]{1,0:T(8,128)S(1)} %copy-done), custom_call_target="tpu_custom_call" | custom-call | tf_op jit(solution)/shard_map/assemble/pallas_call | solution.py:457
Async XLA Ops:
  74.4 0.8 %copy-start = (f32[32,512]{1,0:T(8,128)S(1)}, f32[32,512]{1,0:T(8,128)}, u32[]{:S(2)}) copy-start(f32[32,512]{1,0:T(8,128)} %get-tuple-element.7.cells) | copy-start | bytes 196612
  75.2 0.7 copy-start.1

commit v2 on v1

--- a/solution.py
+++ b/solution.py
@@ -19,16 +19,18 @@
 GROUP = 4
 CHUNK = 256
 ITEMS = (
-    (1, 0), (3, 0), (0, 1), (0, 3), (2, 2), (1, 1), (3, 3), (1, 3),
-    (3, 1), (2, 1), (2, 3), (1, 2), (3, 2), (2, 0), (0, 2),
+    (1, 0), (3, 0), (0, 1), (0, 3), (1, 1), (3, 3), (1, 3), (3, 1),
+    (2, 2), (2, 1), (2, 3), (1, 2), (3, 2), (2, 0), (0, 2),
 )
 CODES = tuple(dz * SIDE + dy for dy, dz in ITEMS)
+RAW = 4
 PARTS = 4
-ORDER = [(p, part) for part in range(PARTS) for p in range(4)]
-ORDER += [(p, part) for part in range(PARTS) for p in range(4, 15)]
-SENT = (16, 24, 28, 32, 36, 40, 44, 48)
-SENT_SORT = 52
-SENT_NARROW = 56
+ORDER = [(p, part) for part in range(PARTS) for p in range(4, 8)]
+ORDER += [(p, part) for part in range(PARTS) for p in range(8, 15)]
+SENT = (16, 22, 25, 28, 31, 34, 36, 38)
+SENT_LAST = 39
+SENT_SORT = 40
+SENT_NARROW = 42
 
 
 def silu(v):
@@ -36,9 +38,9 @@
 
 
 def main_kernel(
-    group_of, state, w_in_hbm, w_out_hbm, w_flux, owner, slot, weight,
+    group_of, state, w_in_hbm, w_out_hbm, w_flux_hbm, owner, slot, weight,
     pool, ocean, sel,
-    xs, ys, send, w_in, w_out, hid, fm, fs, fp, fr, key, jrank, bmat, msg, n1, w2, sl, s1, s1t, s2, hot,
+    xs, rx, ys, send, w_in, w_out, hid, fm, fs, fp, fr, key, jrank, bmat, msg, n1, w2, ahead_of, cells_of, sl, s1, s1t, s2, hot,
     code_t, slot_t, next_t, rank_t, order_t, local_t,
     load_sem, big_s, big_r, fl_s, fl_r, na_s, na_r, wi_s, wi_r, sn_s, sn_r, sw_s, sw_r,
 ):
@@ -46,7 +48,8 @@
     y, z = lax.rem(w, SIDE), lax.div(w, SIDE)
     loads = [
         pltpu.make_async_copy(w_in_hbm, w_in, load_sem.at[0]),
-        pltpu.make_async_copy(w_out_hbm, w_out, load_sem.at[9]),
+        pltpu.make_async_copy(w_out_hbm, w_out.at[pl.ds(0, DEPTH)], load_sem.at[9]),
+        pltpu.make_async_copy(w_flux_hbm, w_out.at[pl.ds(DEPTH, NFLUX)], load_sem.at[10]),
     ]
     for i in range(8):
         loads.append(
@@ -54,10 +57,10 @@
                 state.at[pl.ds(4 * i, 4)], xs.at[pl.ds(4 * i, 4)], load_sem.at[1 + i]
             )
         )
-    loads[0].start()
-    for c in loads[2:]:
+    for c in loads[3:]:
         c.start()
-    loads[1].start()
+    for c in loads[:3]:
+        c.start()
 
     def target(p):
         dy, dz = ITEMS[p]
@@ -93,7 +96,7 @@
         next_t[p] = nxt
         slot_t[p] = jnp.maximum(found[p], 0)
     count = jnp.int32(0)
-    for p in range(15):
+    for p in range(RAW, 15):
         rank_t[p] = jnp.minimum(count, MOVE - 1)
         count = count + jnp.where(found[p] >= 0, 1, 0)
 
@@ -101,7 +104,7 @@
         order_t[k] = slot_t[p]
         return next_t[p + 1]
 
-    lax.fori_loop(0, MOVE, walk_movers, next_t[0])
+    lax.fori_loop(0, MOVE, walk_movers, next_t[RAW])
 
     def back_locals(i, nx):
         s = BLOCKS - 1 - i
@@ -130,8 +133,11 @@
     before = jnp.where(sub < lane, 1.0, 0.0).astype(BF16)
     ones = jnp.full((COLS, COLS), 1.0, BF16)
 
-    def place(i, carry):
-        base, table = carry
+    ahead_of[...] = jnp.zeros((COLS, COLS), F32)
+    cells_of[...] = jnp.zeros((COLS, COLS), F32)
+
+    def place(i):
+        base, table = ahead_of[...], cells_of[...]
         for g in range(4):
             s = 4 * i + g
             o = owner[s]
@@ -142,21 +148,19 @@
             count = jnp.dot(member16, ones, preferred_element_type=F32)
             rank = jnp.sum((ahead + base) * member, axis=0, keepdims=True).astype(I32)
             base = base + count
-            key[s] = row * 16 + (rank >> 2)
-            jrank[s] = rank & 3
+            key[s] = row * 8 + (rank >> 3)
+            jrank[s] = rank & 7
             cell = (slot[s] - SLOTS // 2).astype(F32)
             ranked = jnp.where(sub == rank, cell, 0.0).astype(BF16)
             table = table + lax.dot_general(member16, ranked, NT, preferred_element_type=F32)
-        return base, table
+        ahead_of[...] = base
+        cells_of[...] = table
 
     def slots_out():
-        zero = jnp.zeros((COLS, COLS), F32)
-        _, table = lax.fori_loop(0, BLOCKS // 4, place, (zero, zero))
-        sl[...] = table.reshape(NARROW, WIDE, COLS)
+        sl[...] = cells_of[...].reshape(NARROW, WIDE, COLS)
         for c in slot_narrow:
             c.start()
         s1[n] = sl[n]
-
 
     slot_narrow = []
     for d in range(1, NARROW):
@@ -170,7 +174,7 @@
         rows = pl.ds(0, DEPTH) if part is None else pl.ds(part * CHUNK, CHUNK)
         return pltpu.make_async_remote_copy(
             send.at[p, rows],
-            pool.at[STAY + CODES[p], rows],
+            rx.at[p, rows] if p < RAW else pool.at[STAY + CODES[p], rows],
             big_s.at[p],
             big_r.at[p],
             device_id=target(p),
@@ -202,92 +206,121 @@
             )
         )
 
-    for c in loads:
+    for c in loads[3:]:
         c.wait()
-
-    @pl.loop(0, BLOCKS // GROUP)
-    def _(q):
-        x = jnp.concatenate([xs[order_t[GROUP * q + g]] for g in range(GROUP)], axis=1)
+    for p in range(RAW):
+        send[p] = xs[slot_t[p]]
+    pl.semaphore_wait(barrier, len(wide_peers) + len(narrow_peers))
+    for part in range(PARTS):
+        for p in range(RAW):
+            big(p, part).start()
+    for c in loads[:3]:
+        c.wait()
+
+    def columns(v, g):
+        return v[:, g * COLS : (g + 1) * COLS]
+
+    def compute(x, put_flux, put_rows):
         for m in range(DEPTH // CHUNK):
             rows = pl.ds(m * CHUNK, CHUNK)
             hid[rows, :] = silu(
                 jnp.dot(w_in[rows, :], x, preferred_element_type=F32)
             ).astype(BF16)
         h = hid[...]
-        f = jnp.dot(w_flux[...], h, preferred_element_type=F32)
-
-        @pl.when(q < 2)
-        def _():
+        for m in range(DEPTH // CHUNK):
+            last = m == DEPTH // CHUNK - 1
+            rows = pl.ds(m * CHUNK, CHUNK)
+            both = jnp.dot(
+                w_out[pl.ds(m * CHUNK, CHUNK + (NFLUX if last else 0)), :],
+                h,
+                preferred_element_type=F32,
+            )
+            fresh = both[:CHUNK] + x[m * CHUNK : (m + 1) * CHUNK].astype(F32)
+            put_rows(rows, fresh.astype(BF16))
+            if last:
+                put_flux(both[CHUNK:])
+
+    def gathered(q):
+        return jnp.concatenate([xs[order_t[GROUP * q + g]] for g in range(GROUP)], axis=1)
+
+    def moved(q):
+        def put_flux(f):
             for g in range(GROUP):
-                fm[GROUP * q + g] = f[:, g * COLS : (g + 1) * COLS]
-
-        @pl.when(q >= 2)
-        def _():
+                fm[GROUP * q + g] = columns(f, g)
+
+        def put_rows(rows, fresh):
             for g in range(GROUP):
-                fp[GROUP * q - MOVE + g] = f[:, g * COLS : (g + 1) * COLS]
-
-        for m in range(DEPTH // CHUNK):
-            rows = pl.ds(m * CHUNK, CHUNK)
-            fresh = jnp.dot(w_out[rows, :], h, preferred_element_type=F32)
-            fresh = (fresh + x[m * CHUNK : (m + 1) * CHUNK].astype(F32)).astype(BF16)
-
-            @pl.when(q < 2)
-            def _(rows=rows, fresh=fresh):
-                for g in range(GROUP):
-                    ys[GROUP * q + g, rows] = fresh[:, g * COLS : (g + 1) * COLS]
-
-            @pl.when(q >= 2)
-            def _(rows=rows, fresh=fresh):
-                for g in range(GROUP):
-                    pool[GROUP * q - MOVE + g, rows] = fresh[:, g * COLS : (g + 1) * COLS]
-
-        @pl.when(q == 0)
-        def _():
-            fill(range(4))
-            pl.semaphore_wait(barrier, len(wide_peers) + len(narrow_peers))
-            for p in range(4):
-                flux_copy(p).start()
-            send_big(0, SENT[0])
-
-        @pl.when(q == 1)
-        def _():
-            fill(range(4, 15))
-            for p in range(4, 15):
-                flux_copy(p).start()
-            send_big(SENT[0], SENT[1])
-            slots_out()
-
-        @pl.when(q == 3)
-        def _():
-            for c in slot_narrow:
-                c.wait()
-            for p in range(NARROW):
-                s1t[:, p, :] = s1[p]
-            s2[w] = s1t[w]
-            for c in slot_wide:
-                c.start()
-
-        for step in range(2, BLOCKS // GROUP):
-
-            @pl.when(q == step)
+                ys[GROUP * q + g, rows] = columns(fresh, g)
+
+        place(q)
+        compute(gathered(q), put_flux, put_rows)
+
+    def send_moved(ps, first, last):
+        fill(ps)
+        for p in ps:
+            flux_copy(p).start()
+        send_big(first, last)
+
+    moved(0)
+    send_moved(range(4, 8), 0, SENT[0])
+    moved(1)
+    send_moved(range(8, 15), SENT[0], SENT[1])
+
+    @pl.loop(0, STAY // GROUP)
+    def _(k):
+        def put_flux(f):
+            for g in range(GROUP):
+                fp[GROUP * k + g] = columns(f, g)
+
+        def put_rows(rows, fresh):
+            for g in range(GROUP):
+                pool[GROUP * k + g, rows] = columns(fresh, g)
+
+        place(k + 2)
+        compute(gathered(k + 2), put_flux, put_rows)
+        for step in range(STAY // GROUP):
+
+            @pl.when(k == step)
             def _(step=step):
-                send_big(SENT[step - 1], SENT[step])
-
-
-    for p in range(15):
+                send_big(SENT[step + 1], SENT[step + 2])
+
+    slots_out()
+
+    for p in range(RAW):
+        big(p).wait_recv()
+
+    def raw_flux(f):
+        for p in range(RAW):
+            fp[STAY + CODES[p]] = columns(f, p)
+
+    def raw_rows(rows, fresh):
+        for p in range(RAW):
+            pool[STAY + CODES[p], rows] = columns(fresh, p)
+
+    compute(jnp.concatenate([rx[p] for p in range(RAW)], axis=1), raw_flux, raw_rows)
+
+    for c in slot_narrow:
+        c.wait()
+    for p in range(NARROW):
+        s1t[:, p, :] = s1[p]
+    s2[w] = s1t[w]
+    for c in slot_wide:
+        c.start()
+    send_big(SENT[-1], SENT_LAST)
+
+    for p in range(RAW, 15):
         flux_copy(p).wait()
-    fp[STAY:] = fr[...].astype(F32)
-
-    send_big(SENT[-1], SENT_SORT)
+        fp[STAY + CODES[p]] = fr[CODES[p]].astype(F32)
+    send_big(SENT_LAST, SENT_SORT)
 
     @pl.loop(0, BLOCKS)
     def _(s):
         f = fp[sel[s]] * weight[s]
         j = jrank[s]
-        spread = jnp.concatenate([jnp.where(j == k, f, 0.0) for k in range(4)], axis=0)
+        spread = jnp.concatenate([jnp.where(j == k, f, 0.0) for k in range(8)], axis=0)
         bmat[s] = spread.astype(BF16)
 
-    HALF = WIDE * 16
+    HALF = WIDE * 8
     row_id = lax.broadcasted_iota(I32, (2 * HALF, COLS), 0)
 
     def narrow_copy(d):
@@ -301,7 +334,7 @@
         d = 2 * r + 1
         p0, p1 = lax.rem(n + d, NARROW), lax.rem(n + d + 1, NARROW)
         wanted = row_id + jnp.where(row_id < HALF, p0 * HALF, (p1 - 1) * HALF)
-        acc = jnp.zeros((2 * HALF, COLS), F32)
+        acc = jnp.zeros((2 * HALF, 2 * COLS), F32)
         for b in range(0, BLOCKS, 4):
             pick = jnp.concatenate(
                 [jnp.where(wanted == key[b + g], 1.0, 0.0).astype(BF16) for g in range(4)],
@@ -309,7 +342,9 @@
             )
             vals = jnp.concatenate([bmat[b + g] for g in range(4)], axis=1)
             acc = acc + lax.dot_general(pick, vals, NT, preferred_element_type=F32)
-        both = acc.astype(BF16).reshape(2, WIDE, 16, COLS)
+        low = acc[:, :COLS].reshape(2, WIDE, 8, COLS)
+        high = acc[:, COLS:].reshape(2, WIDE, 8, COLS)
+        both = jnp.concatenate([low, high], axis=2).astype(BF16)
         msg[p0] = both[0]
         msg[p1] = both[1]
         narrow_copy(d).start()
@@ -320,8 +355,6 @@
 
     send_big(SENT_SORT, SENT_NARROW)
     n1[:, n] = msg[n]
-    for c in slot_wide:
-        c.wait()
     for d in range(1, NARROW):
         narrow_copy(d).wait()
     wide = []
@@ -335,6 +368,9 @@
     w2[w] = n1[w]
     send_big(SENT_NARROW, len(ORDER))
 
+    for c in slot_wide:
+        c.wait()
+
     cells = s2[...].reshape(DEVICES, COLS).astype(BF16)
     ROWS = 256
     sub2 = lax.broadcasted_iota(I32, (ROWS, COLS), 0)
@@ -345,7 +381,7 @@
         own = jnp.where(lane2 == r * (ROWS // 16) + (sub2 >> 4), 1.0, 0.0).astype(BF16)
         mine = jnp.dot(own, cells, preferred_element_type=F32)
         for j in range(4):
-            one = jnp.where(lane2 == 4 * (sub2 & 15) + j, mine, 0.0).astype(BF16)
+            one = jnp.where(lane2 == 8 * (sub2 & 7) + 4 * ((sub2 >> 3) & 1) + j, mine, 0.0).astype(BF16)
             cell = jnp.dot(one, ones, preferred_element_type=F32)
             cell = cell.astype(I32) + SLOTS // 2
             for k in range(SLOTS // COLS):
@@ -365,7 +401,9 @@
         )
     ocean[...] = total
 
-    for p in range(15):
+    for p in range(RAW):
+        big(p).wait_send()
+    for p in range(RAW, 15):
         big(p).wait()
 
 
@@ -393,17 +431,18 @@
         main_kernel,
         out_shape=(
             pltpu.VMEM((STAY + WIDE, DEPTH, COLS), BF16),
-            jax.ShapeDtypeStruct((NFLUX, SLOTS), F32),
-            jax.ShapeDtypeStruct((BLOCKS,), I32),
+            pltpu.VMEM((NFLUX, SLOTS), F32),
+            pltpu.SMEM((BLOCKS,), I32),
         ),
-        in_specs=[smem, hbm, hbm, hbm, vmem, vmem, vmem, vmem],
+        in_specs=[smem, hbm, hbm, hbm, hbm, vmem, vmem, vmem],
         out_specs=(vmem, vmem, smem),
         scratch_shapes=[
             pltpu.VMEM((BLOCKS, DEPTH, COLS), BF16),
+            pltpu.VMEM((RAW, DEPTH, COLS), BF16),
             pltpu.VMEM((MOVE, DEPTH, COLS), BF16),
             pltpu.VMEM((15, DEPTH, COLS), BF16),
             pltpu.VMEM((DEPTH, DEPTH), BF16),
-            pltpu.VMEM((DEPTH, DEPTH), BF16),
+            pltpu.VMEM((DEPTH + NFLUX, DEPTH), BF16),
             pltpu.VMEM((DEPTH, GROUP * COLS), BF16),
             pltpu.VMEM((MOVE, NFLUX, COLS), F32),
             pltpu.VMEM((15, NFLUX, COLS), BF16),
@@ -411,10 +450,12 @@
             pltpu.VMEM((WIDE, NFLUX, COLS), BF16),
             pltpu.VMEM((BLOCKS, 1, COLS), I32),
             pltpu.VMEM((BLOCKS, 1, COLS), I32),
-            pltpu.VMEM((BLOCKS, COLS, COLS), BF16),
+            pltpu.VMEM((BLOCKS, 2 * COLS, COLS), BF16),
             pltpu.VMEM((NARROW, WIDE, 16, COLS), BF16),
             pltpu.VMEM((WIDE, NARROW, 16, COLS), BF16),
             pltpu.VMEM((WIDE, NARROW, 16, COLS), BF16),
+            pltpu.VMEM((COLS, COLS), F32),
+            pltpu.VMEM((COLS, COLS), F32),
             pltpu.VMEM((NARROW, WIDE, COLS), F32),
             pltpu.VMEM((NARROW, WIDE, COLS), F32),
             pltpu.VMEM((WIDE, NARROW, COLS), F32),
@@ -426,7 +467,7 @@
             pltpu.SMEM((15,), I32),
             pltpu.SMEM((BLOCKS,), I32),
             pltpu.SMEM((BLOCKS + 1,), I32),
-            dma((10,)),
+            dma((11,)),
             dma((15,)),
             dma((15,)),
             dma((15,)),
@@ -441,7 +482,7 @@
             dma((WIDE,)),
         ],
         compiler_params=pltpu.CompilerParams(
-            collective_id=1, has_side_effects=True, vmem_limit_bytes=49 * 2**20
+            collective_id=1, has_side_effects=True, vmem_limit_bytes=50 * 2**20
         ),
         name="physics",
     )(

time: 80.2 us -> 70.9 us (0.88)
  Pallas kernels: 77.8 us -> 70.1 us
  local copies, waits for them, and re-layouts: 1.51 us -> 0 us
    pallas_call x1, Pallas kernels: 73.7 us -> 66.5 us  [per_device(): pl.pallas_call(main_kernel, out_shape=(pltpu.VMEM((STAY + WIDE, DEPTH, CO...]
    unnamed x4 -> x0, local copies, waits for them, and re-layouts: 1.51 us -> none
where the time goes in v2:
time: 70.9 us; the launch traced here: 70.7 us
  Pallas kernels  70.1 us (99%)
    pallas_call x1, Pallas kernels, per_device(): pl.pallas_call(main_kernel, out_shape=(pltpu.VMEM((STAY + WIDE, DEPTH, CO...  66.5 us
    pallas_call x1, Pallas kernels, per_device(): pl.pallas_call(final_kernel, out_shape=(jax.ShapeDtypeStruct((BLOCKS, DEP...  3.56 us

profile of v2, /device:TPU:1, one launch (start us, length us, event | category | flops | bytes accessed | tf_op | source)
XLA Modules:
  0.0 70.7 jit_solution(17289484625698571371)
XLA Ops:
  0.6 66.5 %physics.1 = (bf16[40,1024,128]{2,1,0:T(8,128)(2,1)S(1)}, f32[32,512]{1,0:T(8,128)S(1)}, s32[32]{0:T(128)S(4)}) custom-call(s32[4096]{0:T(1024)} %group_of.1, bf16[32,1024,128]{2,1,0:T(8,128)(2,1)} %state.1, bf16[1024,1024]{1,0:T(8,128)(2,1)} %w_in_hbm.1, bf16[1024,1024]{1,0:T(8,128)(2,1)} %w_out_hbm.1, bf16[32,1024]{1,0:T(8,128)(2,1)} %w_flux_hbm.1, ...), custom_call_target="tpu_custom_call" | custom-call | tf_op jit(solution)/shard_map/physics/pallas_call | solution.py:430
  67.2 3.6 %assemble.1 = (bf16[32,1024,128]{2,1,0:T(8,128)(2,1)}, f32[32,512]{1,0:T(8,128)}) custom-call(s32[32]{0:T(128)S(4)} %get-tuple-element.5.sel, bf16[40,1024,128]{2,1,0:T(8,128)(2,1)S(1)} %get-tuple-element.6.pool, f32[32,512]{1,0:T(8,128)S(1)} %get-tuple-element.7.cells), custom_call_target="tpu_custom_call" | custom-call | tf_op jit(solution)/shard_map/assemble/pallas_call | solution.py:498

commit v3 on v2

--- a/solution.py
+++ b/solution.py
@@ -18,19 +18,20 @@
 MOVE, STAY = 8, 24
 GROUP = 4
 CHUNK = 256
+PIECE = 128
 ITEMS = (
     (1, 0), (3, 0), (0, 1), (0, 3), (1, 1), (3, 3), (1, 3), (3, 1),
     (2, 2), (2, 1), (2, 3), (1, 2), (3, 2), (2, 0), (0, 2),
 )
 CODES = tuple(dz * SIDE + dy for dy, dz in ITEMS)
 RAW = 4
-PARTS = 4
+PARTS = 8
 ORDER = [(p, part) for part in range(PARTS) for p in range(4, 8)]
 ORDER += [(p, part) for part in range(PARTS) for p in range(8, 15)]
-SENT = (16, 22, 25, 28, 31, 34, 36, 38)
-SENT_LAST = 39
-SENT_SORT = 40
-SENT_NARROW = 42
+SENT = (32, 40, 46, 52, 58, 64, 68, 72)
+SENT_LAST = 74
+SENT_SORT = 76
+SENT_NARROW = 80
 
 
 def silu(v):
@@ -171,7 +172,7 @@
         slot_narrow.append(c)
 
     def big(p, part=None):
-        rows = pl.ds(0, DEPTH) if part is None else pl.ds(part * CHUNK, CHUNK)
+        rows = pl.ds(0, DEPTH) if part is None else pl.ds(part * PIECE, PIECE)
         return pltpu.make_async_remote_copy(
             send.at[p, rows],
             rx.at[p, rows] if p < RAW else pool.at[STAY + CODES[p], rows],

time: 70.9 us -> 69.7 us (0.983)
  Pallas kernels: 70.1 us -> 68.5 us
    pallas_call x1, Pallas kernels: 66.5 us -> 65 us  [per_device(): pl.pallas_call(main_kernel, out_shape=(pltpu.VMEM((STAY + WIDE, DEPTH, CO...]
where the time goes in v3:
time: 69.7 us; the launch traced here: 69.2 us
  Pallas kernels  68.5 us (98%)
    pallas_call x1, Pallas kernels, per_device(): pl.pallas_call(main_kernel, out_shape=(pltpu.VMEM((STAY + WIDE, DEPTH, CO...  65 us
    pallas_call x1, Pallas kernels, per_device(): pl.pallas_call(final_kernel, out_shape=(jax.ShapeDtypeStruct((BLOCKS, DEP...  3.56 us

profile of v3, /device:TPU:1, one launch (start us, length us, event | category | flops | bytes accessed | tf_op | source)
XLA Modules:
  0.0 69.2 jit_solution(17456504849908464146)
XLA Ops:
  0.6 65.0 %physics.1 = (bf16[40,1024,128]{2,1,0:T(8,128)(2,1)S(1)}, f32[32,512]{1,0:T(8,128)S(1)}, s32[32]{0:T(128)S(4)}) custom-call(s32[4096]{0:T(1024)} %group_of.1, bf16[32,1024,128]{2,1,0:T(8,128)(2,1)} %state.1, bf16[1024,1024]{1,0:T(8,128)(2,1)} %w_in_hbm.1, bf16[1024,1024]{1,0:T(8,128)(2,1)} %w_out_hbm.1, bf16[32,1024]{1,0:T(8,128)(2,1)} %w_flux_hbm.1, ...), custom_call_target="tpu_custom_call" | custom-call | tf_op jit(solution)/shard_map/physics/pallas_call | solution.py:431
  65.6 3.6 %assemble.1 = (bf16[32,1024,128]{2,1,0:T(8,128)(2,1)}, f32[32,512]{1,0:T(8,128)}) custom-call(s32[32]{0:T(128)S(4)} %get-tuple-element.5.sel, bf16[40,1024,128]{2,1,0:T(8,128)(2,1)S(1)} %get-tuple-element.6.pool, f32[32,512]{1,0:T(8,128)S(1)} %get-tuple-element.7.cells), custom_call_target="tpu_custom_call" | custom-call | tf_op jit(solution)/shard_map/assemble/pallas_call | solution.py:499
